TPU v7x, 32 devices: a whole 2x2x4 slice. The times are simulated.
32 devices in a mesh: groups: 2 (over x), dp: 2 (over core), tensor: 8 (over z, y).
Axes of the slice: x: 2, y: 2, z: 4, core: 2. Of those that a mesh axis runs over, the one named last changes fastest.
Arguments:
- reward_hidden: bfloat16 [32, 256, 8192], P(('groups', 'dp'), None, 'tensor'), parts along dimension 0, may hold values from -6 to 6
- reward_gain: float32 [8192], P('tensor'), may hold values from 0.5 to 1.5
- reward_head: float32 [8192], P('tensor'), may hold values from -1 to 1
- decode_inputs: bfloat16 [2, 32, 8192], P(None, ('groups', 'dp'), 'tensor'), parts along dimension 1, may hold values from -6 to 6
- attn_gain: float32 [8192], replicated, may hold values from 0.5 to 1.5
- w_query: bfloat16 [8192, 8192], P(None, 'tensor'), may hold values from -0.0625 to 0.0625
- w_keyval: bfloat16 [8192, 2048], P(None, 'tensor'), may hold values from -0.0625 to 0.0625
- w_out: bfloat16 [8192, 8192], P('tensor'), may hold values from -3 to 3
- cache_keys: bfloat16 [32, 2048, 1024], P(('groups', 'dp'), 'tensor'), parts along dimension 0, may hold values from -720 to 720
- cache_values: bfloat16 [32, 2048, 1024], P(('groups', 'dp'), 'tensor'), parts along dimension 0, may hold values from -6 to 6
- lengths: int32 [32], P('groups'), parts along dimension 0, may hold values from 512 to 2048
- slot_map: int32 [32], P('groups'), parts along dimension 0, may hold values from 0 to 15, as said below
Outputs:
- reward: float32 [32], P(('groups', 'dp')), parts along dimension 0
- decoded: bfloat16 [2, 32, 8192], P(None, ('groups', 'dp'), 'tensor'), parts along dimension 1
There are 2 independent parts, one for each index of `groups`. A program takes and returns all parts, laid end to end along the dimension named above; an argument that names none is the same for every part. Nothing has to cross between parts.
Inputs may be any that keep to these rules, and one draw needn't show every extreme that they name: `slot_map`: each aligned block of 8 slots holds exactly 4 survivors, which map to themselves; every other slot maps to a survivor, and every survivor is named by exactly one other slot.
All inputs are finite; a program needn't handle non-finite values.
Results may differ from a plain program's by a relative error of at most 0.0055.
The roundings to bfloat16 on the way count: a program that leaves them out, or rounds other values in their place, can miss the bound.
Values may be sent and summed in bfloat16 or wider, within the bound.
No kernel may reach another device: no remote copies, remote signals or barrier semaphores. Data moves between devices by JAX's collectives and lax.ppermute only.
A program may use at most 128 MiB of HBM per device.

v0:
```python
import jax
import jax.numpy as jnp
from jax import lax
from jax.sharding import PartitionSpec as P

D = 8192
QH = 64
KVH = 8
HD = 128
STEPS = 2
EPS = 1e-05
NEG = -1e30


def fold_sources(parts):
    maxima, totals, sums = parts
    top = jnp.max(maxima, axis=0)
    factor = jnp.exp(maxima - top[None])
    return (top, jnp.sum(factor * totals, axis=0), jnp.sum(factor[..., None] * sums, axis=0))


def local(
    reward_hidden,
    reward_gain,
    reward_head,
    decode_inputs,
    attn_gain,
    w_query,
    w_keyval,
    w_out,
    cache_keys,
    cache_values,
    lengths,
    slot_map,
):
    hidden = reward_hidden.astype(jnp.float32)
    squares = jnp.sum(hidden * hidden, axis=-1)
    head_dot = jnp.sum(hidden * (reward_gain * reward_head), axis=-1)
    squares, head_dot = lax.psum((squares, head_dot), "tensor")
    reward = jnp.mean(head_dot * lax.rsqrt(squares / D + EPS), axis=-1)
    rows = cache_keys.shape[0]
    width = cache_keys.shape[1]
    base = lax.axis_index("dp") * rows
    mine = lax.dynamic_slice_in_dim(slot_map, base, rows)
    every_k, every_v = (
        lax.all_gather(cache_keys, "dp", axis=0, tiled=True),
        lax.all_gather(cache_values, "dp", axis=0, tiled=True),
    )
    keys_now = jnp.take(every_k, mine, axis=0)
    values_now = jnp.take(every_v, mine, axis=0)
    live = jnp.take(lengths, mine, axis=0)
    group = QH // KVH
    heads_dev = w_query.shape[1] // HD
    keys4 = keys_now.reshape(rows, width, KVH, HD)
    values4 = values_now.reshape(rows, width, KVH, HD)
    positions = lax.axis_index("tensor") * width + jnp.arange(width)
    valid = (positions[None, :] < live[:, None])[:, None, None, :]
    head_start = lax.axis_index("tensor") * heads_dev
    kv_index = (head_start + jnp.arange(heads_dev)) // group
    scale = HD ** (-0.5)
    new_keys = []
    new_values = []
    outputs = []
    for step in range(STEPS):
        whole = lax.all_gather(decode_inputs[step], "tensor", axis=1, tiled=True).astype(
            jnp.float32
        )
        normed = (
            whole * lax.rsqrt(jnp.mean(whole * whole, axis=-1, keepdims=True) + EPS) * attn_gain
        ).astype(jnp.bfloat16)
        query_part = jnp.dot(normed, w_query, preferred_element_type=jnp.float32).astype(
            jnp.bfloat16
        )
        kv_part = jnp.dot(normed, w_keyval, preferred_element_type=jnp.float32).astype(jnp.bfloat16)
        query_all, keyval = (
            lax.all_gather(query_part, "tensor", axis=1, tiled=True),
            lax.all_gather(kv_part, "tensor", axis=1, tiled=True),
        )
        query = query_all.reshape(rows, KVH, group, HD)
        keyval = keyval.reshape(rows, 2, KVH, HD)
        new_keys.append(keyval[:, 0])
        new_values.append(keyval[:, 1])
        scores = (
            jnp.einsum("rkgd,rwkd->rkgw", query, keys4, preferred_element_type=jnp.float32) * scale
        )
        scores = jnp.where(valid, scores, NEG)
        block_max = jnp.max(scores, axis=-1)
        expo = jnp.where(valid, jnp.exp(scores - block_max[..., None]), 0.0)
        block_total = jnp.sum(expo, axis=-1).reshape(rows, QH)
        block_acc = jnp.einsum(
            "rkgw,rwkd->rkgd",
            expo.astype(jnp.bfloat16),
            values4,
            preferred_element_type=jnp.float32,
        )
        block_acc = block_acc.reshape(rows, QH, HD)
        block_max = block_max.reshape(rows, QH)
        cache_top, cache_total, cache_acc = fold_sources(
            (
                lax.all_to_all(block_max[None], "tensor", split_axis=2, concat_axis=0, tiled=True),
                lax.all_to_all(
                    block_total[None], "tensor", split_axis=2, concat_axis=0, tiled=True
                ),
                lax.all_to_all(block_acc[None], "tensor", split_axis=2, concat_axis=0, tiled=True),
            )
        )
        query_own = query_part.reshape(rows, heads_dev, HD)
        fresh_k = jnp.take(jnp.stack(new_keys, axis=1), kv_index, axis=2)
        fresh_v = jnp.take(jnp.stack(new_values, axis=1), kv_index, axis=2)
        recent = (
            jnp.einsum("rhd,rjhd->rhj", query_own, fresh_k, preferred_element_type=jnp.float32)
            * scale
        )
        recent_max = jnp.max(recent, axis=-1)
        recent_exp = jnp.exp(recent - recent_max[..., None])
        recent_total = jnp.sum(recent_exp, axis=-1)
        recent_acc = jnp.einsum(
            "rhj,rjhd->rhd",
            recent_exp.astype(jnp.bfloat16),
            fresh_v,
            preferred_element_type=jnp.float32,
        )
        top = jnp.maximum(cache_top, recent_max)
        cache_factor = jnp.exp(cache_top - top)
        recent_factor = jnp.exp(recent_max - top)
        total = cache_factor * cache_total + recent_factor * recent_total
        acc = cache_factor[..., None] * cache_acc + recent_factor[..., None] * recent_acc
        attended = (acc / total[..., None]).astype(jnp.bfloat16).reshape(rows, heads_dev * HD)
        partial_out = jnp.dot(attended, w_out, preferred_element_type=jnp.float32)
        summed = lax.psum_scatter(partial_out, "tensor", scatter_dimension=1, tiled=True)
        outputs.append(summed.astype(jnp.bfloat16))
    return (reward, jnp.stack(outputs, axis=0))


def solution(mesh):
    return jax.shard_map(
        local,
        mesh=mesh,
        in_specs=(
            P(("groups", "dp"), None, "tensor"),
            P("tensor"),
            P("tensor"),
            P(None, ("groups", "dp"), "tensor"),
            P(),
            P(None, "tensor"),
            P(None, "tensor"),
            P("tensor", None),
            P(("groups", "dp"), "tensor", None),
            P(("groups", "dp"), "tensor", None),
            P("groups"),
            P("groups"),
        ),
        out_specs=(P(("groups", "dp")), P(None, ("groups", "dp"), "tensor")),
        check_vma=False,
    )
```

profile of v0, /device:TPU:0, one launch (start us, length us, event | category | flops | bytes accessed | tf_op | source)
XLA Modules:
  0.0 486.0 jit_solution(13673014890106930044)
XLA Ops:
  8.7 32.3 %all-gather = bf16[1,8,8192]{2,1,0:T(8,128)(2,1)S(1)} all-gather(bf16[1,8,1024]{2,1,0:T(8,128)(2,1)S(1)} %get-tuple-element.26), channel_id=2, replica_groups=mesh['groups'=2,'dp'=2,'tensor'=8] {'tensor'}, dimensions={2}, use_global_device_ids=true | all-gather | bytes 147456 | tf_op jit(solution)/shard_map/all_gather | solution.py:65
  41.2 3.5 convolution_convert_fusion.3
  44.8 30.6 %all_gather.27 = bf16[8,2048]{1,0:T(8,128)(2,1)S(1)} all-gather(bf16[8,256]{1,0:T(8,128)(2,1)S(1)} %convolution_convert_fusion.3), channel_id=1, replica_groups=mesh['groups'=2,'dp'=2,'tensor'=8] {'tensor'}, dimensions={1}, use_global_device_ids=true | all-gather | bytes 36864 | tf_op jit(solution)/shard_map/all_gather | solution.py:77
  76.0 8.2 %fusion.61 = (f32[8,8]{0,1:T(8,128)S(1)}, bf16[8,1024]{1,0:T(8,128)(2,1)S(1)}) fusion(bf16[8,8,128]{2,1,0:T(8,128)(2,1)S(1)} %gather_fusion.2, pred[8]{0:T(512)(128)(4,1)S(1)} %compare_and_fusion, bf16[8192,1024]{1,0:T(8,128)(2,1)} %param.23, bf16[1,8,8192]{2,1,0:T(8,128)(2,1)S(1)} %all-gather, f32[8192]{0:T(1024)S(1)} %copy-done.2, f32[8]{0:T(128)S(1)} %add_rsqrt_fusion.1), kind=kOutput, calls=%fused_computation.78 | convolution fusion | flops 134528960 | bytes 16974120 | tf_op jit(solution)/shard_map/dot_general | solution.py:71
  84.8 30.5 %all-gather.1 = bf16[1,8,8192]{2,1,0:T(8,128)(2,1)S(1)} all-gather(bf16[1,8,1024]{2,1,0:T(8,128)(2,1)S(1)} %get-tuple-element.27), channel_id=3, replica_groups=mesh['groups'=2,'dp'=2,'tensor'=8] {'tensor'}, dimensions={2}, use_global_device_ids=true | all-gather | bytes 147456 | tf_op jit(solution)/shard_map/all_gather | solution.py:65
  118.4 30.6 %all_gather.31 = bf16[8,2048]{1,0:T(8,128)(2,1)S(1)} all-gather(bf16[8,256]{1,0:T(8,128)(2,1)S(1)} %convolution_convert_fusion.2), channel_id=1, replica_groups=mesh['groups'=2,'dp'=2,'tensor'=8] {'tensor'}, dimensions={1}, use_global_device_ids=true | all-gather | bytes 36864 | tf_op jit(solution)/shard_map/all_gather | solution.py:77
  150.3 8.1 %convolution_convert_fusion = bf16[8,1024]{1,0:T(8,128)(2,1)S(1)} fusion(bf16[8192,1024]{1,0:T(8,128)(2,1)} %param.23, bf16[1,8,8192]{2,1,0:T(8,128)(2,1)S(1)} %all-gather.1, f32[8]{0:T(128)S(1)} %add_rsqrt_fusion, f32[8192]{0:T(1024)S(1)} %copy-done.2), kind=kOutput, calls=%fused_computation.31 | convolution fusion | flops 134488064 | bytes 16957472 | tf_op jit(solution)/shard_map/dot_general | solution.py:71
  159.8 3.6 fusion.1
  163.5 37.1 %all-reduce = (f32[8,256]{1,0:T(8,128)S(1)}, f32[8,256]{1,0:T(8,128)S(1)}) all-reduce(f32[8,256]{1,0:T(8,128)S(1)} %get-tuple-element.6, f32[8,256]{1,0:T(8,128)S(1)} %get-tuple-element.4), channel_id=1, replica_groups=mesh['groups'=2,'dp'=2,'tensor'=8] {'tensor'}, use_global_device_ids=true, to_apply=%region_1.0 | all-reduce | flops 4096 | bytes 32768 | tf_op jit(solution)/shard_map/psum | solution.py:39
  200.5 30.5 %all_gather.30 = bf16[8,8192]{1,0:T(8,128)(2,1)S(1)} all-gather(bf16[8,1024]{1,0:T(8,128)(2,1)S(1)} %convolution_convert_fusion), channel_id=1, replica_groups=mesh['groups'=2,'dp'=2,'tensor'=8] {'tensor'}, dimensions={1}, use_global_device_ids=true | all-gather | bytes 147456 | tf_op jit(solution)/shard_map/all_gather | solution.py:76
  231.0 30.7 %all_gather.25 = bf16[8,8192]{1,0:T(8,128)(2,1)S(1)} all-gather(bf16[8,1024]{1,0:T(8,128)(2,1)S(1)} %get-tuple-element.43), channel_id=1, replica_groups=mesh['groups'=2,'dp'=2,'tensor'=8] {'tensor'}, dimensions={1}, use_global_device_ids=true | all-gather | bytes 147456 | tf_op jit(solution)/shard_map/all_gather | solution.py:76
  262.0 6.1 %gather_fusion.1 = bf16[8,256,1024]{2,1,0:T(8,128)(2,1)} fusion(bf16[16,256,1024]{2,1,0:T(8,128)(2,1)} %all-gather.5.cloned.1.call-done, s32[1024]{0:T(1024)S(1)} %pad_clamp_fusion.1), kind=kCustom, calls=%fused_computation.clone | custom fusion | bytes 8388640 | tf_op jit(solution)/shard_map/jit(_take)/gather | solution.py:49
  268.2 6.2 %gather_fusion.3 = bf16[8,256,1024]{2,1,0:T(8,128)(2,1)} fusion(bf16[16,256,1024]{2,1,0:T(8,128)(2,1)} %all-gather.7.cloned.1.call-done, s32[1024]{0:T(1024)S(1)} %pad_clamp_fusion.1), kind=kCustom, calls=%fused_computation.3.clone | custom fusion | bytes 8388640 | tf_op jit(solution)/shard_map/jit(_take)/gather | solution.py:50
  274.3 6.2 %select_bitcast_fusion.1 = (bf16[8,32,8,8,128]{4,3,2,1,0:T(8,128)(2,1)S(1)}, bf16[8,32,8,8,128]{4,3,2,1,0:T(8,128)(2,1)}) fusion(bf16[8,256,1024]{2,1,0:T(8,128)(2,1)} %gather_fusion.1, pred[8]{0:T(512)(128)(4,1)S(1)} %get-tuple-element.18, bf16[8,256,1024]{2,1,0:T(8,128)(2,1)} %gather_fusion.3), kind=kLoop, calls=%fused_computation.20 | loop fusion | flops 4194304 | bytes 16777224
  303.9 5.4 %all-to-all-start.5 = ((f32[1,8,64]{1,0,2:T(1,128)}), f32[1,8,64]{1,0,2:T(1,128)S(1)}, u32[]{:S(2)}, u32[]{:S(2)}) async-start(f32[1,8,64]{1,0,2:T(1,128)} %bitcast.47), calls=%async_computation.6 | async-start | bytes 65536 | tf_op jit(solution)/shard_map/all_to_all | solution.py:101
  309.4 6.6 %all-to-all-done.5 = f32[1,8,64]{1,0,2:T(1,128)S(1)} async-done(((f32[1,8,64]{1,0,2:T(1,128)}), f32[1,8,64]{1,0,2:T(1,128)S(1)}, u32[]{:S(2)}, u32[]{:S(2)}) %all-to-all-start.5) | async-done | bytes 2080 | tf_op jit(solution)/shard_map/all_to_all | solution.py:101
  319.4 6.6 %all-to-all-done.3 = f32[1,8,64]{1,0,2:T(1,128)S(1)} async-done(((f32[1,8,64]{1,0,2:T(1,128)}), f32[1,8,64]{1,0,2:T(1,128)S(1)}, u32[]{:S(2)}, u32[]{:S(2)}) %all-to-all-start.3) | async-done | bytes 2080 | tf_op jit(solution)/shard_map/all_to_all | solution.py:100
  325.9 3.4 all-to-all-start.1
  329.7 7.8 %all-to-all-done.1 = f32[1,8,64,128]{3,1,0,2:T(8,128)S(1)} async-done(((f32[1,8,64,128]{3,1,0,2:T(8,128)}), f32[1,8,64,128]{3,1,0,2:T(8,128)S(1)}, u32[]{:S(2)}, u32[]{:S(2)}) %all-to-all-start.1) | async-done | bytes 262176 | tf_op jit(solution)/shard_map/all_to_all | solution.py:104
  337.5 3.4 all-to-all-start.4
  341.1 8.8 %fusion.75 = f32[8,8192]{1,0:T(8,128)} fusion(bf16[1024,8192]{1,0:T(8,128)(2,1)} %param.25, f32[8,8,128]{2,1,0:T(8,128)S(1)} %fusion.44, bf16[8,8,128]{2,1,0:T(8,128)(2,1)S(1)} %gather_fusion.4, f32[8,8]{0,1:T(8,128)S(1)} %copy.125, f32[8,8]{0,1:T(8,128)S(1)} %copy.122, f32[8,8]{0,1:T(8,128)S(1)} %copy.121, f32[8,8]{0,1:T(8,128)S(1)} %copy.116, ...), kind=kOutput, calls=%fused_computation.96 | convolution fusion | flops 134283264 | bytes 17089544 | tf_op jit(solution)/shard_map/dot_general | solution.py:129
  350.2 8.8 %fusion.73 = f32[8,8192]{1,0:T(8,128)} fusion(bf16[1024,8192]{1,0:T(8,128)(2,1)} %param.25, f32[8,8,1,128]{3,2,1,0:T(1,128)S(1)} %fusion.63, f32[8,8,128]{2,0,1:T(8,128)S(1)} %multiply_reduce_fusion, f32[8,8]{0,1:T(8,128)S(1)} %get-tuple-element.13, f32[8,8]{0,1:T(8,128)S(1)} %get-tuple-element.15, f32[8,8]{0,1:T(8,128)S(1)} %get-tuple-element.14), kind=kOutput, calls=%fused_computation.94 | convolution fusion | flops 134258688 | bytes 17105664 | tf_op jit(solution)/shard_map/dot_general | solution.py:129
  359.6 53.8 %reduce-scatter.3.cloned.1.call-done = f32[8,1024]{1,0:T(8,128)} async-done(((f32[8,8192]{1,0:T(8,128)}), f32[8,1024]{1,0:T(8,128)}) %reduce-scatter.3.cloned.1.call-update) | async-done | bytes 32784 | tf_op jit(solution)/shard_map/reduce_scatter | solution.py:130
  414.2 63.9 %reduce-scatter.5.cloned.1.call-done = f32[8,1024]{1,0:T(8,128)} async-done(((f32[8,8192]{1,0:T(8,128)}), f32[8,1024]{1,0:T(8,128)}) %reduce-scatter.5.cloned.1.call-update) | async-done | bytes 32784 | tf_op jit(solution)/shard_map/reduce_scatter | solution.py:130
  (93 shorter events, 39.1 us)
Async XLA Ops:
  7.2 152.0 %copy-start = (s32[16]{0:T(128)S(1)}, s32[16]{0:T(128)}, u32[]{:S(2)}) copy-start(s32[16]{0:T(128)} %param.28) | copy-start | bytes 196
  7.2 1.5 copy-start.3
  7.2 34.1 %copy-start.2 = (f32[8192]{0:T(1024)S(1)}, f32[8192]{0:T(1024)}, u32[]{:S(2)}) copy-start(f32[8192]{0:T(1024)} %param.22) | copy-start | bytes 98308
  7.2 254.8 %all-gather.5.cloned.1.call-start = ((), (), s32[]{:S(2)}) async-start(), calls=%async_computation.8 | async-start | bytes 12582912 | tf_op jit(solution)/shard_map/all_gather | solution.py:46
  7.9 260.2 %all-gather.7.cloned.1.call-start = ((), (), s32[]{:S(2)}) async-start(), calls=%async_computation.9 | async-start | bytes 12582912 | tf_op jit(solution)/shard_map/all_gather | solution.py:47
  150.3 8.8 %copy-start.6 = (s32[16]{0:T(128)S(1)}, s32[16]{0:T(128)}, u32[]{:S(2)}) copy-start(s32[16]{0:T(128)} %param.29) | copy-start | bytes 196
  150.3 9.5 %copy-start.4 = (f32[1024]{0:T(1024)S(1)}, f32[1024]{0:T(1024)}, u32[]{:S(2)}) copy-start(f32[1024]{0:T(1024)} %param.19) | copy-start | bytes 12292
  150.3 9.5 %copy-start.5 = (f32[1024]{0:T(1024)S(1)}, f32[1024]{0:T(1024)}, u32[]{:S(2)}) copy-start(f32[1024]{0:T(1024)} %param.20) | copy-start | bytes 12292
  283.8 10.1 %all-to-all-start = ((f32[1,8,64]{1,0,2:T(1,128)}), f32[1,8,64]{1,0,2:T(1,128)S(1)}, u32[]{:S(2)}, u32[]{:S(2)}) async-start(f32[1,8,64]{1,0,2:T(1,128)} %bitcast.3), calls=%async_computation | async-start | bytes 65536 | tf_op jit(solution)/shard_map/all_to_all | solution.py:100
  293.9 10.0 %all-to-all-start.2 = ((f32[1,8,64]{1,0,2:T(1,128)}), f32[1,8,64]{1,0,2:T(1,128)S(1)}, u32[]{:S(2)}, u32[]{:S(2)}) async-start(f32[1,8,64]{1,0,2:T(1,128)} %bitcast.21), calls=%async_computation.2 | async-start | bytes 65536 | tf_op jit(solution)/shard_map/all_to_all | solution.py:101
  303.9 12.1 %all-to-all-start.5 = ((f32[1,8,64]{1,0,2:T(1,128)}), f32[1,8,64]{1,0,2:T(1,128)S(1)}, u32[]{:S(2)}, u32[]{:S(2)}) async-start(f32[1,8,64]{1,0,2:T(1,128)} %bitcast.47), calls=%async_computation.6 | async-start | bytes 65536 | tf_op jit(solution)/shard_map/all_to_all | solution.py:101
  316.0 10.0 %all-to-all-start.3 = ((f32[1,8,64]{1,0,2:T(1,128)}), f32[1,8,64]{1,0,2:T(1,128)S(1)}, u32[]{:S(2)}, u32[]{:S(2)}) async-start(f32[1,8,64]{1,0,2:T(1,128)} %bitcast.30), calls=%async_computation.4 | async-start | bytes 65536 | tf_op jit(solution)/shard_map/all_to_all | solution.py:100
  325.9 11.6 %all-to-all-start.1 = ((f32[1,8,64,128]{3,1,0,2:T(8,128)}), f32[1,8,64,128]{3,1,0,2:T(8,128)S(1)}, u32[]{:S(2)}, u32[]{:S(2)}) async-start(f32[1,8,64,128]{3,1,0,2:T(8,128)} %copy.118), calls=%async_computation.1 | async-start | bytes 524288 | tf_op jit(solution)/shard_map/all_to_all | solution.py:104
  337.5 12.5 %all-to-all-start.4 = ((f32[1,8,64,128]{3,1,0,2:T(8,128)}), f32[1,8,64,128]{3,1,0,2:T(8,128)S(1)}, u32[]{:S(2)}, u32[]{:S(2)}) async-start(f32[1,8,64,128]{3,1,0,2:T(8,128)} %copy.131), calls=%async_computation.5 | async-start | bytes 524288 | tf_op jit(solution)/shard_map/all_to_all | solution.py:104
  340.9 72.5 %reduce-scatter.3.cloned.1.call-start = ((), (), s32[]{:S(2)}) async-start(), calls=%async_computation.10 | async-start | bytes 294912 | tf_op jit(solution)/shard_map/reduce_scatter | solution.py:130
  349.9 128.2 %reduce-scatter.5.cloned.1.call-start = ((), (), s32[]{:S(2)}) async-start(), calls=%async_computation.11 | async-start | bytes 294912 | tf_op jit(solution)/shard_map/reduce_scatter | solution.py:130
  350.1 129.3 %copy-start.1 = (s32[16]{0:T(128)S(1)}, s32[16]{0:T(128)}, u32[]{:S(2)}) copy-start(s32[16]{0:T(128)} %param.28) | copy-start | bytes 196
Sparse Core Ops, SparseCore 0:
  9.5 22.5 all-gather.4
  33.7 21.0 all-gather.6
  350.1 63.3 reduce-scatter.2
  416.6 61.4 reduce-scatter.4
where the time goes:
time: 487 us; the launch traced here: 486 us
  blocking collectives  222 us (46%)
  waiting for transfers between devices  143 us (29%)
  matrix products  49 us (10%)
  starting transfers between devices  22.4 us (5%)
  local copies, waits for them, and re-layouts  20.7 us (4%)
  other arithmetic  14.1 us (3%)
  between operations  14.1 us (3%)
    reduce_scatter x2, waiting for transfers between devices, local(): lax.psum_scatter(partial_out, 'tensor', scatter_dimension=1, tiled=True)  118 us
    all_gather x2, blocking collectives, local(): lax.all_gather(decode_inputs[step], 'tensor', axis=1, tiled=True)  62.9 us
    all_gather x2, blocking collectives, local(): lax.all_gather(kv_part, 'tensor', axis=1, tiled=True)  61.2 us
    all_gather x2, blocking collectives, local(): lax.all_gather(query_part, 'tensor', axis=1, tiled=True)  61.2 us
    psum x1, blocking collectives, local(): squares, head_dot = lax.psum((squares, head_dot), 'tensor')  37.1 us
    dot_general x2, matrix products, local(): partial_out = jnp.dot(attended, w_out, preferred_element_type=jnp.float32)  17.6 us
    dot_general x2, matrix products, local(): jnp.dot(normed, w_query, preferred_element_type=jnp.float32)  16.2 us
  transfers between devices with their start and end apart: 10, of which 7 were waited for; matrix products, arithmetic and copies ran while one was open for 14% of the time, Pallas kernels for 0%

commit v1 on v0

--- a/solution.py
+++ b/solution.py
@@ -10,6 +10,11 @@
 STEPS = 2
 EPS = 1e-05
 NEG = -1e30
+
+
+def exchange_gather(shard, axis, d):
+    sent = jnp.stack([shard] * lax.axis_size(axis))
+    return jnp.concatenate(lax.all_to_all(sent, axis, 0, 0), axis=d)
 
 
 def fold_sources(parts):
@@ -73,7 +78,7 @@
         )
         kv_part = jnp.dot(normed, w_keyval, preferred_element_type=jnp.float32).astype(jnp.bfloat16)
         query_all, keyval = (
-            lax.all_gather(query_part, "tensor", axis=1, tiled=True),
+            exchange_gather(query_part, "tensor", 1),
             lax.all_gather(kv_part, "tensor", axis=1, tiled=True),
         )
         query = query_all.reshape(rows, KVH, group, HD)

time: 487 us -> 447 us (0.918)
  blocking collectives: 222 us -> 162 us
  starting transfers between devices: 22.4 us -> 31.5 us
    all_gather x2 -> x0, blocking collectives: 61.2 us -> none  [local(): lax.all_gather(query_part, 'tensor', axis=1, tiled=True)]
    all_to_all x0 -> x2, starting transfers between devices: none -> 9.05 us  [exchange_gather(): return jnp.concatenate(lax.all_to_all(sent, axis, 0, 0), axis=d)]
  transfers between devices with their start and end apart: 10 -> 12, of which waited for: 7 -> 8; matrix products, arithmetic and copies ran while one was open for 14% -> 19% of each run, Pallas kernels for 0% -> 0%
where the time goes in v1:
time: 447 us; the launch traced here: 445 us
  blocking collectives  162 us (36%)
  waiting for transfers between devices  147 us (33%)
  matrix products  53.4 us (12%)
  starting transfers between devices  31.5 us (7%)
  local copies, waits for them, and re-layouts  22 us (5%)
  other arithmetic  15.4 us (3%)
  between operations  14.1 us (3%)
    reduce_scatter x2, waiting for transfers between devices, local(): lax.psum_scatter(partial_out, 'tensor', scatter_dimension=1, tiled=True)  118 us
    all_gather x2, blocking collectives, local(): lax.all_gather(decode_inputs[step], 'tensor', axis=1, tiled=True)  63.4 us
    all_gather x2, blocking collectives, local(): lax.all_gather(kv_part, 'tensor', axis=1, tiled=True)  61.2 us
    psum x1, blocking collectives, local(): squares, head_dot = lax.psum((squares, head_dot), 'tensor')  37 us
    dot_general x2, matrix products, local(): partial_out = jnp.dot(attended, w_out, preferred_element_type=jnp.float32)  17.6 us
    dot_general x2, matrix products, local(): jnp.dot(normed, w_query, preferred_element_type=jnp.float32)  16.2 us
    all_to_all x2, waiting for transfers between devices, local(): lax.all_to_all(block_max[None], 'tensor', split_axis=2, concat_axis=0, ti...  9.28 us
    all_to_all x2, starting transfers between devices, exchange_gather(): return jnp.concatenate(lax.all_to_all(sent, axis, 0, 0), axis=d)  9.05 us
  transfers between devices with their start and end apart: 12, of which 8 were waited for; matrix products, arithmetic and copies ran while one was open for 19% of the time, Pallas kernels for 0%

profile of v1, /device:TPU:0, one launch (start us, length us, event | category | flops | bytes accessed | tf_op | source)
XLA Modules:
  0.0 445.1 jit_solution(6229577311912191280)
XLA Ops:
  8.7 32.3 %all-gather = bf16[1,8,8192]{2,1,0:T(8,128)(2,1)S(1)} all-gather(bf16[1,8,1024]{2,1,0:T(8,128)(2,1)S(1)} %get-tuple-element.26), channel_id=2, replica_groups=mesh['groups'=2,'dp'=2,'tensor'=8] {'tensor'}, dimensions={2}, use_global_device_ids=true | all-gather | bytes 147456 | tf_op jit(solution)/shard_map/all_gather | solution.py:70
  41.2 3.5 convolution_convert_fusion.3
  44.8 30.6 %all_gather.20 = bf16[8,2048]{1,0:T(8,128)(2,1)S(1)} all-gather(bf16[8,256]{1,0:T(8,128)(2,1)S(1)} %convolution_convert_fusion.3), channel_id=1, replica_groups=mesh['groups'=2,'dp'=2,'tensor'=8] {'tensor'}, dimensions={1}, use_global_device_ids=true | all-gather | bytes 36864 | tf_op jit(solution)/shard_map/all_gather | solution.py:82
  76.0 8.2 %fusion.61 = (f32[8,8]{0,1:T(8,128)S(1)}, bf16[8,1024]{1,0:T(8,128)(2,1)S(1)}) fusion(bf16[8,8,128]{2,1,0:T(8,128)(2,1)S(1)} %gather_fusion.2, pred[8]{0:T(512)(128)(4,1)S(1)} %compare_and_fusion, bf16[8192,1024]{1,0:T(8,128)(2,1)} %param.23, bf16[1,8,8192]{2,1,0:T(8,128)(2,1)S(1)} %all-gather, f32[8192]{0:T(1024)S(1)} %copy-done.2, f32[8]{0:T(128)S(1)} %add_rsqrt_fusion.1), kind=kOutput, calls=%fused_computation.80 | convolution fusion | flops 134528960 | bytes 16974120 | tf_op jit(solution)/shard_map/dot_general | solution.py:76
  84.8 5.5 %all-to-all-start = ((bf16[8,8,1024]{2,1,0:T(8,128)(2,1)}), bf16[8,8,1024]{2,1,0:T(8,128)(2,1)S(1)}, u32[]{:S(2)}, u32[]{:S(2)}) async-start(bf16[8,8,1024]{2,1,0:T(8,128)(2,1)} %stack.14), calls=%async_computation | async-start | bytes 262144 | tf_op jit(solution)/shard_map/all_to_all | solution.py:17
  91.0 31.1 %all-gather.1 = bf16[1,8,8192]{2,1,0:T(8,128)(2,1)S(1)} all-gather(bf16[1,8,1024]{2,1,0:T(8,128)(2,1)S(1)} %get-tuple-element.27), channel_id=3, replica_groups=mesh['groups'=2,'dp'=2,'tensor'=8] {'tensor'}, dimensions={2}, use_global_device_ids=true | all-gather | bytes 147456 | tf_op jit(solution)/shard_map/all_gather | solution.py:70
  125.1 30.6 %all_gather.23 = bf16[8,2048]{1,0:T(8,128)(2,1)S(1)} all-gather(bf16[8,256]{1,0:T(8,128)(2,1)S(1)} %convolution_convert_fusion.2), channel_id=1, replica_groups=mesh['groups'=2,'dp'=2,'tensor'=8] {'tensor'}, dimensions={1}, use_global_device_ids=true | all-gather | bytes 36864 | tf_op jit(solution)/shard_map/all_gather | solution.py:82
  157.0 8.1 %convolution_convert_fusion = bf16[8,1024]{1,0:T(8,128)(2,1)S(1)} fusion(bf16[8192,1024]{1,0:T(8,128)(2,1)} %param.23, bf16[1,8,8192]{2,1,0:T(8,128)(2,1)S(1)} %all-gather.1, f32[8]{0:T(128)S(1)} %add_rsqrt_fusion, f32[8192]{0:T(1024)S(1)} %copy-done.2), kind=kOutput, calls=%fused_computation.31 | convolution fusion | flops 134488064 | bytes 16957472 | tf_op jit(solution)/shard_map/dot_general | solution.py:76
  166.5 3.6 fusion.1
  170.2 37.0 %all-reduce = (f32[8,256]{1,0:T(8,128)S(1)}, f32[8,256]{1,0:T(8,128)S(1)}) all-reduce(f32[8,256]{1,0:T(8,128)S(1)} %get-tuple-element.6, f32[8,256]{1,0:T(8,128)S(1)} %get-tuple-element.4), channel_id=1, replica_groups=mesh['groups'=2,'dp'=2,'tensor'=8] {'tensor'}, use_global_device_ids=true, to_apply=%region_1.0 | all-reduce | flops 4096 | bytes 32768 | tf_op jit(solution)/shard_map/psum | solution.py:44
  207.5 6.1 %gather_fusion.1 = bf16[8,256,1024]{2,1,0:T(8,128)(2,1)} fusion(bf16[16,256,1024]{2,1,0:T(8,128)(2,1)} %all-gather.5.cloned.1.call-done, s32[1024]{0:T(1024)S(1)} %pad_clamp_fusion.1), kind=kCustom, calls=%fused_computation.clone | custom fusion | bytes 8388640 | tf_op jit(solution)/shard_map/jit(_take)/gather | solution.py:54
  213.6 6.2 %gather_fusion.3 = bf16[8,256,1024]{2,1,0:T(8,128)(2,1)} fusion(bf16[16,256,1024]{2,1,0:T(8,128)(2,1)} %all-gather.7.cloned.1.call-done, s32[1024]{0:T(1024)S(1)} %pad_clamp_fusion.1), kind=kCustom, calls=%fused_computation.3.clone | custom fusion | bytes 8388640 | tf_op jit(solution)/shard_map/jit(_take)/gather | solution.py:55
  219.8 7.5 %select_bitcast_fusion.1 = (bf16[8,32,8,8,128]{4,3,2,1,0:T(8,128)(2,1)}, bf16[8,32,8,8,128]{4,3,2,1,0:T(8,128)(2,1)}) fusion(bf16[8,256,1024]{2,1,0:T(8,128)(2,1)} %gather_fusion.1, pred[8]{0:T(512)(128)(4,1)S(1)} %get-tuple-element.18, bf16[8,256,1024]{2,1,0:T(8,128)(2,1)} %gather_fusion.3), kind=kLoop, calls=%fused_computation.20 | loop fusion | flops 4194304 | bytes 16777224
  227.9 3.5 all-to-all-start.4
  231.5 3.5 fusion.105
  234.9 3.8 all-to-all-done.4
  263.0 5.4 %all-to-all-start.7 = ((f32[1,8,64]{1,0,2:T(1,128)}), f32[1,8,64]{1,0,2:T(1,128)S(1)}, u32[]{:S(2)}, u32[]{:S(2)}) async-start(f32[1,8,64]{1,0,2:T(1,128)} %bitcast.47), calls=%async_computation.8 | async-start | bytes 65536 | tf_op jit(solution)/shard_map/all_to_all | solution.py:106
  268.5 6.6 %all-to-all-done.7 = f32[1,8,64]{1,0,2:T(1,128)S(1)} async-done(((f32[1,8,64]{1,0,2:T(1,128)}), f32[1,8,64]{1,0,2:T(1,128)S(1)}, u32[]{:S(2)}, u32[]{:S(2)}) %all-to-all-start.7) | async-done | bytes 2080 | tf_op jit(solution)/shard_map/all_to_all | solution.py:106
  278.4 6.6 %all-to-all-done.5 = f32[1,8,64]{1,0,2:T(1,128)S(1)} async-done(((f32[1,8,64]{1,0,2:T(1,128)}), f32[1,8,64]{1,0,2:T(1,128)S(1)}, u32[]{:S(2)}, u32[]{:S(2)}) %all-to-all-start.5) | async-done | bytes 2080 | tf_op jit(solution)/shard_map/all_to_all | solution.py:105
  288.8 7.8 %all-to-all-done.2 = f32[1,8,64,128]{3,1,0,2:T(8,128)S(1)} async-done(((f32[1,8,64,128]{3,1,0,2:T(8,128)}), f32[1,8,64,128]{3,1,0,2:T(8,128)S(1)}, u32[]{:S(2)}, u32[]{:S(2)}) %all-to-all-start.2) | async-done | bytes 262176 | tf_op jit(solution)/shard_map/all_to_all | solution.py:109
  300.2 8.8 %fusion.75 = f32[8,8192]{1,0:T(8,128)} fusion(bf16[1024,8192]{1,0:T(8,128)(2,1)} %param.25, f32[8,8,128]{2,1,0:T(8,128)S(1)} %fusion.44, bf16[8,8,128]{2,1,0:T(8,128)(2,1)S(1)} %gather_fusion.4, f32[8,8]{0,1:T(8,128)S(1)} %copy.121, f32[8,8]{0,1:T(8,128)S(1)} %copy.118, f32[8,8]{0,1:T(8,128)S(1)} %copy.117, f32[8,8]{0,1:T(8,128)S(1)} %copy.112, ...), kind=kOutput, calls=%fused_computation.98 | convolution fusion | flops 134283264 | bytes 17089544 | tf_op jit(solution)/shard_map/dot_general | solution.py:134
  309.3 8.8 %fusion.73 = f32[8,8192]{1,0:T(8,128)} fusion(bf16[1024,8192]{1,0:T(8,128)(2,1)} %param.25, f32[8,8,1,128]{3,2,1,0:T(1,128)S(1)} %fusion.63, f32[8,8,128]{2,0,1:T(8,128)S(1)} %multiply_reduce_fusion, f32[8,8]{0,1:T(8,128)S(1)} %get-tuple-element.13, f32[8,8]{0,1:T(8,128)S(1)} %get-tuple-element.15, f32[8,8]{0,1:T(8,128)S(1)} %get-tuple-element.14), kind=kOutput, calls=%fused_computation.96 | convolution fusion | flops 134258688 | bytes 17105664 | tf_op jit(solution)/shard_map/dot_general | solution.py:134
  318.7 53.8 %reduce-scatter.3.cloned.1.call-done = f32[8,1024]{1,0:T(8,128)} async-done(((f32[8,8192]{1,0:T(8,128)}), f32[8,1024]{1,0:T(8,128)}) %reduce-scatter.3.cloned.1.call-update) | async-done | bytes 32784 | tf_op jit(solution)/shard_map/reduce_scatter | solution.py:135
  373.3 63.9 %reduce-scatter.5.cloned.1.call-done = f32[8,1024]{1,0:T(8,128)} async-done(((f32[8,8192]{1,0:T(8,128)}), f32[8,1024]{1,0:T(8,128)}) %reduce-scatter.5.cloned.1.call-update) | async-done | bytes 32784 | tf_op jit(solution)/shard_map/reduce_scatter | solution.py:135
  (97 shorter events, 48.2 us)
Async XLA Ops:
  7.2 158.7 %copy-start = (s32[16]{0:T(128)S(1)}, s32[16]{0:T(128)}, u32[]{:S(2)}) copy-start(s32[16]{0:T(128)} %param.28) | copy-start | bytes 196
  7.2 1.5 copy-start.3
  7.2 34.0 %copy-start.2 = (f32[8192]{0:T(1024)S(1)}, f32[8192]{0:T(1024)}, u32[]{:S(2)}) copy-start(f32[8192]{0:T(1024)} %param.22) | copy-start | bytes 98308
  7.2 200.3 %all-gather.5.cloned.1.call-start = ((), (), s32[]{:S(2)}) async-start(), calls=%async_computation.10 | async-start | bytes 12582912 | tf_op jit(solution)/shard_map/all_gather | solution.py:51
  7.9 205.7 %all-gather.7.cloned.1.call-start = ((), (), s32[]{:S(2)}) async-start(), calls=%async_computation.11 | async-start | bytes 12582912 | tf_op jit(solution)/shard_map/all_gather | solution.py:52
  84.8 142.4 %all-to-all-start = ((bf16[8,8,1024]{2,1,0:T(8,128)(2,1)}), bf16[8,8,1024]{2,1,0:T(8,128)(2,1)S(1)}, u32[]{:S(2)}, u32[]{:S(2)}) async-start(bf16[8,8,1024]{2,1,0:T(8,128)(2,1)} %stack.14), calls=%async_computation | async-start | bytes 262144 | tf_op jit(solution)/shard_map/all_to_all | solution.py:17
  157.0 8.8 %copy-start.6 = (s32[16]{0:T(128)S(1)}, s32[16]{0:T(128)}, u32[]{:S(2)}) copy-start(s32[16]{0:T(128)} %param.29) | copy-start | bytes 196
  157.0 9.5 %copy-start.4 = (f32[1024]{0:T(1024)S(1)}, f32[1024]{0:T(1024)}, u32[]{:S(2)}) copy-start(f32[1024]{0:T(1024)} %param.19) | copy-start | bytes 12292
  157.0 9.5 %copy-start.5 = (f32[1024]{0:T(1024)S(1)}, f32[1024]{0:T(1024)}, u32[]{:S(2)}) copy-start(f32[1024]{0:T(1024)} %param.20) | copy-start | bytes 12292
  227.9 10.8 %all-to-all-start.4 = ((bf16[8,8,1024]{2,1,0:T(8,128)(2,1)}), bf16[8,8,1024]{2,1,0:T(8,128)(2,1)S(1)}, u32[]{:S(2)}, u32[]{:S(2)}) async-start(bf16[8,8,1024]{2,1,0:T(8,128)(2,1)} %stack.16), calls=%async_computation.5 | async-start | bytes 262144 | tf_op jit(solution)/shard_map/all_to_all | solution.py:17
  242.9 10.1 %all-to-all-start.1 = ((f32[1,8,64]{1,0,2:T(1,128)}), f32[1,8,64]{1,0,2:T(1,128)S(1)}, u32[]{:S(2)}, u32[]{:S(2)}) async-start(f32[1,8,64]{1,0,2:T(1,128)} %bitcast.3), calls=%async_computation.1 | async-start | bytes 65536 | tf_op jit(solution)/shard_map/all_to_all | solution.py:105
  253.0 10.0 %all-to-all-start.3 = ((f32[1,8,64]{1,0,2:T(1,128)}), f32[1,8,64]{1,0,2:T(1,128)S(1)}, u32[]{:S(2)}, u32[]{:S(2)}) async-start(f32[1,8,64]{1,0,2:T(1,128)} %bitcast.21), calls=%async_computation.3 | async-start | bytes 65536 | tf_op jit(solution)/shard_map/all_to_all | solution.py:106
  263.0 12.1 %all-to-all-start.7 = ((f32[1,8,64]{1,0,2:T(1,128)}), f32[1,8,64]{1,0,2:T(1,128)S(1)}, u32[]{:S(2)}, u32[]{:S(2)}) async-start(f32[1,8,64]{1,0,2:T(1,128)} %bitcast.47), calls=%async_computation.8 | async-start | bytes 65536 | tf_op jit(solution)/shard_map/all_to_all | solution.py:106
  275.1 10.0 %all-to-all-start.5 = ((f32[1,8,64]{1,0,2:T(1,128)}), f32[1,8,64]{1,0,2:T(1,128)S(1)}, u32[]{:S(2)}, u32[]{:S(2)}) async-start(f32[1,8,64]{1,0,2:T(1,128)} %bitcast.30), calls=%async_computation.6 | async-start | bytes 65536 | tf_op jit(solution)/shard_map/all_to_all | solution.py:105
  285.0 11.6 %all-to-all-start.2 = ((f32[1,8,64,128]{3,1,0,2:T(8,128)}), f32[1,8,64,128]{3,1,0,2:T(8,128)S(1)}, u32[]{:S(2)}, u32[]{:S(2)}) async-start(f32[1,8,64,128]{3,1,0,2:T(8,128)} %copy.114), calls=%async_computation.2 | async-start | bytes 524288 | tf_op jit(solution)/shard_map/all_to_all | solution.py:109
  296.6 12.5 %all-to-all-start.6 = ((f32[1,8,64,128]{3,1,0,2:T(8,128)}), f32[1,8,64,128]{3,1,0,2:T(8,128)S(1)}, u32[]{:S(2)}, u32[]{:S(2)}) async-start(f32[1,8,64,128]{3,1,0,2:T(8,128)} %copy.127), calls=%async_computation.7 | async-start | bytes 524288 | tf_op jit(solution)/shard_map/all_to_all | solution.py:109
  300.0 72.5 %reduce-scatter.3.cloned.1.call-start = ((), (), s32[]{:S(2)}) async-start(), calls=%async_computation.12 | async-start | bytes 294912 | tf_op jit(solution)/shard_map/reduce_scatter | solution.py:135
  309.0 128.2 %reduce-scatter.5.cloned.1.call-start = ((), (), s32[]{:S(2)}) async-start(), calls=%async_computation.13 | async-start | bytes 294912 | tf_op jit(solution)/shard_map/reduce_scatter | solution.py:135
  309.2 129.4 %copy-start.1 = (s32[16]{0:T(128)S(1)}, s32[16]{0:T(128)}, u32[]{:S(2)}) copy-start(s32[16]{0:T(128)} %param.28) | copy-start | bytes 196
Sparse Core Ops, SparseCore 0:
  9.5 22.5 all-gather.4
  33.7 21.0 all-gather.6
  309.2 63.3 reduce-scatter.2
  375.7 61.4 reduce-scatter.4
